TPU v7x, 128 devices: a whole 4x4x4 slice. The times are simulated.
128 devices in a mesh: outer: 8 (over y, core), inner: 16 (over z, x).
Axes of the slice: x: 4, y: 4, z: 4, core: 2. Of those that a mesh axis runs over, the one named last changes fastest.
Arguments:
- layer_input: bfloat16 [16384, 7168], P(('outer', 'inner')), may hold values from -6 to 6
- out_grad: bfloat16 [16384, 7168], P(('outer', 'inner')), may hold values from -3 to 3
- expert_ids: int32 [16384, 8], P(('outer', 'inner')), may hold values from 0 to 255, as said below
- route_scales: float32 [16384, 8], P(('outer', 'inner')), may hold values from 0.25 to 2.5
- w_gate: bfloat16 [8, 7168, 2048], P('outer', None, 'inner'), may hold values from -0.0625 to 0.0625
- w_up: bfloat16 [8, 7168, 2048], P('outer', None, 'inner'), may hold values from -0.0625 to 0.0625
- w_down: bfloat16 [8, 2048, 7168], P('outer', 'inner'), may hold values from -0.125 to 0.125
Outputs:
- in_grad: bfloat16 [16384, 7168], P(('outer', 'inner'))
- grad_w_gate: float32 [8, 7168, 2048], P('outer', None, 'inner')
- grad_w_up: float32 [8, 7168, 2048], P('outer', None, 'inner')
- grad_w_down: float32 [8, 2048, 7168], P('outer', 'inner')
Inputs may be any that keep to these rules, and one draw needn't show every extreme that they name: `expert_ids`: each row names 8 different experts. In each device's aligned block of 128 rows at most 6 rows name any one expert below 8, and in every draw one expert below 8 is named by exactly 6 rows of every block.
All inputs are finite; a program needn't handle non-finite values.
Results may differ from a plain program's by a relative error of at most 0.014.
Values may be sent and summed in bfloat16 or wider, within the bound.
A program may use at most 192 MiB of HBM per device.

v0:
```python
import jax
import jax.numpy as jnp
from jax import lax
from jax.sharding import PartitionSpec as P

CAP = 6


def shards(layer_input, out_grad, expert_ids, route_scales, w_gate, w_up, w_down):
    tok_count = layer_input.shape[0]
    model_width = layer_input.shape[1]
    n_outer = lax.axis_size("outer")
    top_count = expert_ids.shape[1]
    slot_count = n_outer * CAP
    route_ids = expert_ids.reshape(-1)
    onehot = (route_ids[:, None] == jnp.arange(n_outer, dtype=jnp.int32)[None, :]).astype(jnp.int32)
    position = jnp.sum((jnp.cumsum(onehot, axis=0) - onehot) * onehot, axis=1)
    slot = jnp.where(route_ids < n_outer, route_ids * CAP + position, -1)
    picks = slot[:, None] == jnp.arange(slot_count, dtype=jnp.int32)[None, :]
    place = jnp.any(picks.reshape(tok_count, top_count, slot_count), axis=1).astype(jnp.bfloat16)
    slot_scale = jnp.sum(jnp.where(picks, route_scales.reshape(-1)[:, None], 0.0), axis=0)
    take_rows = (((0,), (0,)), ((), ()))
    send_x = lax.dot_general(
        place, layer_input, take_rows, preferred_element_type=jnp.float32
    ).astype(jnp.bfloat16)
    send_dy = lax.dot_general(place, out_grad, take_rows, preferred_element_type=jnp.float32)
    routed = (send_dy * slot_scale[:, None]).astype(jnp.bfloat16)
    send_x = send_x.reshape(n_outer, CAP, model_width)
    routed = routed.reshape(n_outer, CAP, model_width)
    gate_w = w_gate[0]
    up_w = w_up[0]
    down_w = w_down[0]
    got_x, got_gy = (
        lax.all_to_all(send_x, "outer", split_axis=0, concat_axis=0, tiled=True),
        lax.all_to_all(routed, "outer", split_axis=0, concat_axis=0, tiled=True),
    )
    rows_x = lax.all_gather(got_x.reshape(-1, model_width), "inner", axis=0, tiled=True)
    rows_gy = lax.all_gather(got_gy.reshape(-1, model_width), "inner", axis=0, tiled=True)
    gate = jnp.dot(rows_x, gate_w, preferred_element_type=jnp.float32)
    up_val = jnp.dot(rows_x, up_w, preferred_element_type=jnp.float32)
    sigmoid_gate = jax.nn.sigmoid(gate)
    silu_gate = gate * sigmoid_gate
    act = (silu_gate * up_val).astype(jnp.bfloat16)
    hid_grad = lax.dot_general(
        rows_gy, down_w, (((1,), (1,)), ((), ())), preferred_element_type=jnp.float32
    )
    gate_grad = (hid_grad * up_val * sigmoid_gate * (1.0 + gate * (1.0 - sigmoid_gate))).astype(
        jnp.bfloat16
    )
    up_grad = (hid_grad * silu_gate).astype(jnp.bfloat16)
    gate_sum = lax.dot_general(rows_x, gate_grad, take_rows, preferred_element_type=jnp.float32)
    up_sum = lax.dot_general(rows_x, up_grad, take_rows, preferred_element_type=jnp.float32)
    down_sum = lax.dot_general(act, rows_gy, take_rows, preferred_element_type=jnp.float32)
    gate_store = gate_grad
    up_store = up_grad
    carry = (gate_sum, up_sum, down_sum, gate_store, up_store)
    grad_gate, grad_up, grad_down, gate_store, up_store = carry
    term = lax.dot_general(
        gate_store, gate_w, (((1,), (1,)), ((), ())), preferred_element_type=jnp.float32
    )
    mine = lax.psum_scatter(
        (
            term
            + lax.dot_general(
                up_store, up_w, (((1,), (1,)), ((), ())), preferred_element_type=jnp.float32
            )
        ).astype(jnp.bfloat16),
        "inner",
        scatter_dimension=0,
        tiled=True,
    ).astype(jnp.float32)
    mine = mine.astype(jnp.bfloat16).reshape(n_outer, CAP, model_width)
    back = lax.all_to_all(mine, "outer", split_axis=0, concat_axis=0, tiled=True).reshape(
        slot_count, model_width
    )
    in_grad = jnp.dot(place, back, preferred_element_type=jnp.float32).astype(jnp.bfloat16)
    return (in_grad, grad_gate[None], grad_up[None], grad_down[None])


def solution(mesh):
    return jax.shard_map(
        shards,
        mesh=mesh,
        in_specs=(
            P(("outer", "inner"), None),
            P(("outer", "inner"), None),
            P(("outer", "inner"), None),
            P(("outer", "inner"), None),
            P("outer", None, "inner"),
            P("outer", None, "inner"),
            P("outer", "inner", None),
        ),
        out_specs=(
            P(("outer", "inner"), None),
            P("outer", None, "inner"),
            P("outer", None, "inner"),
            P("outer", "inner", None),
        ),
        check_vma=False,
    )
```

profile of v0, /device:TPU:1, one launch (start us, length us, event | category | flops | bytes accessed | tf_op | source)
XLA Modules:
  0.0 355.3 jit_solution(1478537319193128124)
XLA Ops:
  7.2 0.0 copy-start
  7.2 0.0 all-gather.5.cloned.1.call-start
  7.2 0.9 copy.27
  8.1 0.1 eq.45
  8.2 0.1 eq.49
  8.3 2.3 reduce-window.6
  10.6 0.3 slice_reduce_fusion
  10.9 0.2 reduce-window.9
  11.1 0.1 add_bitcast_fusion
  11.2 0.1 reduce_sum.21
  11.3 0.7 add_select_fusion.1
  12.0 0.0 copy-start.4
  12.1 1.9 convolution_convert_fusion.1
  14.0 0.2 reshape.72
  14.2 19.7 %all_to_all.15 = bf16[8,6,7168]{2,1,0:T(8,128)(2,1)} all-to-all(bf16[8,6,7168]{2,1,0:T(8,128)(2,1)S(1)} %reshape.72), channel_id=1, replica_groups=mesh['outer'=8,'inner'=16] {'outer'}, dimensions={0} | all-to-all | bytes 1376256 | tf_op jit(solution)/shard_map/all_to_all | solution.py:34
  33.9 2.3 reshape.73
  36.2 0.0 all-gather.5.cloned.1.call-update
  36.2 0.0 all-gather.3.cloned.1.call-start
  36.2 0.0 copy-done.4
  36.2 0.1 copy.30
  36.3 0.1 broadcast_in_dim.35
  36.4 0.1 select_reduce_fusion
  36.6 1.9 fusion
  38.5 0.2 reshape.70
  38.7 17.8 %all_to_all.16 = bf16[8,6,7168]{2,1,0:T(8,128)(2,1)} all-to-all(bf16[8,6,7168]{2,1,0:T(8,128)(2,1)S(1)} %reshape.70), channel_id=1, replica_groups=mesh['outer'=8,'inner'=16] {'outer'}, dimensions={0} | all-to-all | bytes 1376256 | tf_op jit(solution)/shard_map/all_to_all | solution.py:35
  56.5 2.3 reshape.71
  58.7 0.0 all-gather.3.cloned.1.call-update
  58.8 0.0 reduce-scatter.2.cloned.1.call-start
  58.8 61.0 %all-gather.5.cloned.1.call-done = bf16[768,7168]{1,0:T(8,128)(2,1)} async-done(((bf16[48,7168]{1,0:T(8,128)(2,1)}), bf16[768,7168]{1,0:T(8,128)(2,1)}) %all-gather.5.cloned.1.call-update) | async-done | bytes 11010064 | tf_op jit(solution)/shard_map/all_gather | solution.py:37
  119.8 0.0 copy-done
  119.8 7.2 %fusion.3 = f32[768,128]{1,0:T(8,128)S(1)} fusion(bf16[768,7168]{1,0:T(8,128)(2,1)} %all-gather.5.cloned.1.call-done, bf16[1,7168,128]{2,1,0:T(8,128)(2,1)S(1)} %copy-done), kind=kOutput, calls=%fused_computation.10 | convolution fusion | flops 1409286144 | bytes 13238272 | tf_op jit(solution)/shard_map/dot_general | solution.py:39
  127.0 0.1 copy-done.2
  127.1 0.5 copy-done.3
  127.6 3.0 fusion.6
  130.6 74.4 %all-gather.3.cloned.1.call-done = bf16[768,7168]{1,0:T(8,128)(2,1)} async-done(((bf16[48,7168]{1,0:T(8,128)(2,1)}), bf16[768,7168]{1,0:T(8,128)(2,1)}) %all-gather.3.cloned.1.call-update) | async-done | bytes 11010064 | tf_op jit(solution)/shard_map/all_gather | solution.py:38
  205.0 7.6 %multiply_convert_fusion.1 = (bf16[768,128]{1,0:T(8,128)(2,1)S(1)}, bf16[768,128]{1,0:T(8,128)(2,1)S(1)}) fusion(f32[768,128]{1,0:T(8,128)S(1)} %fusion.3, f32[768,128]{1,0:T(8,128)S(1)} %fusion.6, bf16[768,7168]{1,0:T(8,128)(2,1)} %all-gather.3.cloned.1.call-done, bf16[1,128,7168]{2,1,0:T(8,128)(2,1)} %param.13), kind=kOutput, calls=%fused_computation.18 | convolution fusion | flops 1410564096 | bytes 14024704 | tf_op jit(solution)/shard_map/dot_general | solution.py:44
  212.7 9.0 %fusion.1 = f32[768,7168]{1,0:T(8,128)} fusion(bf16[768,128]{1,0:T(8,128)(2,1)S(1)} %get-tuple-element.5, bf16[1,7168,128]{2,1,0:T(8,128)(2,1)S(1)} %copy-done), kind=kOutput, calls=%fused_computation.8 | convolution fusion | flops 1409286144 | bytes 24051712 | tf_op jit(solution)/shard_map/dot_general | solution.py:58
  221.7 13.2 %add_convert_fusion = bf16[768,7168]{1,0:T(8,128)(2,1)} fusion(f32[768,7168]{1,0:T(8,128)} %fusion.1, bf16[768,128]{1,0:T(8,128)(2,1)S(1)} %get-tuple-element.4, bf16[1,7168,128]{2,1,0:T(8,128)(2,1)} %param.12), kind=kOutput, calls=%fused_computation | convolution fusion | flops 1420296192 | bytes 35061760 | tf_op jit(solution)/shard_map/dot_general | solution.py:64
  234.9 0.0 reduce-scatter.2.cloned.1.call-update
  234.9 9.0 %convolution_bitcast_fusion.1 = f32[1,7168,128]{2,1,0:T(8,128)} fusion(bf16[768,7168]{1,0:T(8,128)(2,1)} %all-gather.5.cloned.1.call-done, bf16[768,128]{1,0:T(8,128)(2,1)S(1)} %get-tuple-element.4), kind=kOutput, calls=%fused_computation.2 | convolution fusion | flops 1409286144 | bytes 14876672 | tf_op jit(solution)/shard_map/dot_general | solution.py:52
  243.9 9.2 %convolution_bitcast_fusion.2 = f32[1,7168,128]{2,1,0:T(8,128)} fusion(bf16[768,7168]{1,0:T(8,128)(2,1)} %all-gather.5.cloned.1.call-done, bf16[768,128]{1,0:T(8,128)(2,1)S(1)} %get-tuple-element.5), kind=kOutput, calls=%fused_computation.3 | convolution fusion | flops 1409286144 | bytes 14876672 | tf_op jit(solution)/shard_map/dot_general | solution.py:51
  253.1 72.1 %reduce-scatter.2.cloned.1.call-done = bf16[48,7168]{1,0:T(8,128)(2,1)} async-done(((bf16[768,7168]{1,0:T(8,128)(2,1)}), bf16[48,7168]{1,0:T(8,128)(2,1)}) %reduce-scatter.2.cloned.1.call-update) | async-done | bytes 688144 | tf_op jit(solution)/shard_map/reduce_scatter | solution.py:61
  325.1 2.3 reshape.74
  327.4 5.5 %all-to-all-start.2 = ((bf16[8,6,7168]{2,1,0:T(8,128)(2,1)}), bf16[8,6,7168]{2,1,0:T(8,128)(2,1)S(1)}, u32[]{:S(2)}, u32[]{:S(2)}) async-start(bf16[8,6,7168]{2,1,0:T(8,128)(2,1)} %reshape.74), calls=%async_computation.3 | async-start | bytes 1835008 | tf_op jit(solution)/shard_map/all_to_all | solution.py:73
  332.9 7.8 %convolution_bitcast_fusion = f32[1,128,7168]{2,1,0:T(8,128)} fusion(bf16[768,7168]{1,0:T(8,128)(2,1)} %all-gather.3.cloned.1.call-done, f32[768,128]{1,0:T(8,128)S(1)} %fusion.6, f32[768,128]{1,0:T(8,128)S(1)} %fusion.3), kind=kOutput, calls=%fused_computation.1 | convolution fusion | flops 1409875968 | bytes 15466496 | tf_op jit(solution)/shard_map/dot_general | solution.py:53
  340.7 5.9 %all-to-all-done.2 = bf16[8,6,7168]{2,1,0:T(8,128)(2,1)S(1)} async-done(((bf16[8,6,7168]{2,1,0:T(8,128)(2,1)}), bf16[8,6,7168]{2,1,0:T(8,128)(2,1)S(1)}, u32[]{:S(2)}, u32[]{:S(2)}) %all-to-all-start.2) | async-done | bytes 688160 | tf_op jit(solution)/shard_map/all_to_all | solution.py:73
  346.6 0.3 reshape.75
  346.8 1.9 convolution_convert_fusion
  (9 shorter events, 0.1 us)
Async XLA Ops:
  7.2 112.6 %copy-start = (bf16[1,7168,128]{2,1,0:T(8,128)(2,1)S(1)}, bf16[1,7168,128]{2,1,0:T(8,128)(2,1)}, u32[]{:S(2)}) copy-start(bf16[1,7168,128]{2,1,0:T(8,128)(2,1)} %param.11) | copy-start | bytes 5505028
  7.2 112.6 %all-gather.5.cloned.1.call-start = ((), (), s32[]{:S(2)}) async-start(), calls=%async_computation.5 | async-start | bytes 11698176 | tf_op jit(solution)/shard_map/all_gather | solution.py:37
  12.0 24.2 %copy-start.4 = (f32[128,8]{0,1:T(8,128)S(1)}, f32[128,8]{0,1:T(8,128)}, u32[]{:S(2)}) copy-start(f32[128,8]{0,1:T(8,128)} %param.10) | copy-start | bytes 12292
  36.2 168.8 %all-gather.3.cloned.1.call-start = ((), (), s32[]{:S(2)}) async-start(), calls=%async_computation.4 | async-start | bytes 11698176 | tf_op jit(solution)/shard_map/all_gather | solution.py:38
  58.8 266.4 %reduce-scatter.2.cloned.1.call-start = ((), (), s32[]{:S(2)}) async-start(), calls=%async_computation.6 | async-start | bytes 11698176 | tf_op jit(solution)/shard_map/reduce_scatter | solution.py:61
  119.8 7.3 %copy-start.2 = (bf16[768,7168]{1,0:T(8,128)(2,1)S(1)}, bf16[768,7168]{1,0:T(8,128)(2,1)}, u32[]{:S(2)}) copy-start(bf16[768,7168]{1,0:T(8,128)(2,1)} %all-gather.5.cloned.1.call-done) | copy-start | bytes 33030148
  119.8 7.8 %copy-start.3 = (bf16[1,7168,128]{2,1,0:T(8,128)(2,1)S(1)}, bf16[1,7168,128]{2,1,0:T(8,128)(2,1)}, u32[]{:S(2)}) copy-start(bf16[1,7168,128]{2,1,0:T(8,128)(2,1)} %param.12) | copy-start | bytes 5505028
  327.4 19.2 %all-to-all-start.2 = ((bf16[8,6,7168]{2,1,0:T(8,128)(2,1)}), bf16[8,6,7168]{2,1,0:T(8,128)(2,1)S(1)}, u32[]{:S(2)}, u32[]{:S(2)}) async-start(bf16[8,6,7168]{2,1,0:T(8,128)(2,1)} %reshape.74), calls=%async_computation.3 | async-start | bytes 1835008 | tf_op jit(solution)/shard_map/all_to_all | solution.py:73
  332.9 15.9 %copy-start.1 = (bf16[1,7168,128]{2,1,0:T(8,128)(2,1)S(1)}, bf16[1,7168,128]{2,1,0:T(8,128)(2,1)}, u32[]{:S(2)}) copy-start(bf16[1,7168,128]{2,1,0:T(8,128)(2,1)} %param.11) | copy-start | bytes 5505028
Sparse Core Ops, SparseCore 0:
  36.3 83.4 all-gather.4
  122.5 82.4 all-gather.2
  235.0 90.0 reduce-scatter.1
where the time goes:
time: 356 us; the launch traced here: 355 us
  waiting for transfers between devices  213 us (60%)
  matrix products  71.7 us (20%)
  blocking collectives  37.4 us (11%)
  between operations  13.9 us (4%)
  local copies, waits for them, and re-layouts  9.88 us (3%)
  starting transfers between devices  5.58 us (2%)
    all_gather x1, waiting for transfers between devices, shards(): lax.all_gather(got_gy.reshape(-1, model_width), 'inner', axis=0, tiled=True)  74.4 us
    reduce_scatter x1, waiting for transfers between devices, shards(): lax.psum_scatter((term + lax.dot_general(up_store, up_w, (((1,), (1,)), (...  72.1 us
    all_gather x1, waiting for transfers between devices, shards(): lax.all_gather(got_x.reshape(-1, model_width), 'inner', axis=0, tiled=True)  61 us
    all_to_all x1, blocking collectives, shards(): lax.all_to_all(send_x, 'outer', split_axis=0, concat_axis=0, tiled=True)  19.7 us
    all_to_all x1, blocking collectives, shards(): lax.all_to_all(routed, 'outer', split_axis=0, concat_axis=0, tiled=True)  17.8 us
    dot_general x1, matrix products, shards(): lax.dot_general(up_store, up_w, (((1,), (1,)), ((), ())), preferred_eleme...  13.2 us
    dot_general x1, matrix products, shards(): lax.dot_general(rows_x, gate_grad, take_rows, preferred_element_type=jnp....  9.15 us
    dot_general x1, matrix products, shards(): lax.dot_general(rows_x, up_grad, take_rows, preferred_element_type=jnp.fl...  9.03 us
  transfers between devices with their start and end apart: 4, of which 4 were waited for; matrix products, arithmetic and copies ran while one was open for 12% of the time, Pallas kernels for 0%

commit v1 on v0

--- a/solution.py
+++ b/solution.py
@@ -4,6 +4,12 @@
 from jax.sharding import PartitionSpec as P
 
 CAP = 6
+
+
+def joined_along(blocks, dim):
+    blocks = jnp.moveaxis(blocks, 0, dim)
+    shape = blocks.shape
+    return blocks.reshape(*shape[:dim], shape[dim] * shape[dim + 1], *shape[dim + 2 :])
 
 
 def shards(layer_input, out_grad, expert_ids, route_scales, w_gate, w_up, w_down):
@@ -34,7 +40,20 @@
         lax.all_to_all(send_x, "outer", split_axis=0, concat_axis=0, tiled=True),
         lax.all_to_all(routed, "outer", split_axis=0, concat_axis=0, tiled=True),
     )
-    rows_x = lax.all_gather(got_x.reshape(-1, model_width), "inner", axis=0, tiled=True)
+    array = got_x.reshape(-1, model_width)
+    size = lax.axis_size("inner")
+    pairs = [(i, (i + 1) % size) for i in range(size)]
+    back_2 = [(b, a) for a, b in pairs]
+    lower, upper = ([], [])
+    for lap in range(size - 1):
+        if lap % 2 == 0:
+            lower.append(lax.ppermute(lower[-1] if lower else array, "inner", pairs))
+        else:
+            upper.append(lax.ppermute(upper[-1] if upper else array, "inner", back_2))
+    pieces = jnp.stack([*lower[::-1], array, *upper])
+    shift = lax.axis_index("inner") - len(lower)
+    pieces = pieces[(jnp.arange(size) - shift) % size]
+    rows_x = joined_along(pieces, 0)
     rows_gy = lax.all_gather(got_gy.reshape(-1, model_width), "inner", axis=0, tiled=True)
     gate = jnp.dot(rows_x, gate_w, preferred_element_type=jnp.float32)
     up_val = jnp.dot(rows_x, up_w, preferred_element_type=jnp.float32)

time: 356 us -> 426 us (1.20)
  starting transfers between devices: 5.58 us -> 53 us
  local copies, waits for them, and re-layouts: 9.88 us -> 48.7 us
  blocking collectives: 37.4 us -> 19.8 us
    ppermute x0 -> x15, waiting for transfers between devices: none -> 87.5 us  [the longest x8 87.5 us: shards(): lower.append(lax.ppermute(lower[-1] if lower else array, 'inner', pairs))]
    all_gather x1 -> x0, waiting for transfers between devices: 61 us -> none  [shards(): lax.all_gather(got_x.reshape(-1, model_width), 'inner', axis=0, tiled=True)]
    all_gather x1, waiting for transfers between devices: 74.4 us -> 35.5 us  [shards(): lax.all_gather(got_gy.reshape(-1, model_width), 'inner', axis=0, tiled=True)]
    ppermute x0 -> x15, starting transfers between devices: none -> 36.2 us  [the longest x7 34.9 us: shards(): upper.append(lax.ppermute(upper[-1] if upper else array, 'inner', back_2))]
    unnamed x12 -> x51, local copies, waits for them, and re-layouts: 1.63 us -> 29 us
    all_to_all x1 -> x0, blocking collectives: 17.8 us -> none  [shards(): lax.all_to_all(routed, 'outer', split_axis=0, concat_axis=0, tiled=True)]
    all_to_all x0 -> x1, waiting for transfers between devices: none -> 13.8 us  [shards(): lax.all_to_all(routed, 'outer', split_axis=0, concat_axis=0, tiled=True)]
    all_to_all x0 -> x1, starting transfers between devices: none -> 11.2 us  [shards(): lax.all_to_all(routed, 'outer', split_axis=0, concat_axis=0, tiled=True)]
  transfers between devices with their start and end apart: 4 -> 19, of which waited for: 4 -> 11; matrix products, arithmetic and copies ran while one was open for 12% -> 18% of each run, Pallas kernels for 0% -> 0%
where the time goes in v1:
time: 426 us; the launch traced here: 425 us
  waiting for transfers between devices  215 us (50%)
  matrix products  71.5 us (17%)
  starting transfers between devices  53 us (12%)
  local copies, waits for them, and re-layouts  48.7 us (11%)
  blocking collectives  19.8 us (5%)
  between operations  14.3 us (3%)
    ppermute x8, waiting for transfers between devices, shards(): lower.append(lax.ppermute(lower[-1] if lower else array, 'inner', pairs))  87.5 us
    reduce_scatter x1, waiting for transfers between devices, shards(): lax.psum_scatter((term + lax.dot_general(up_store, up_w, (((1,), (1,)), (...  71.7 us
    all_gather x1, waiting for transfers between devices, shards(): lax.all_gather(got_gy.reshape(-1, model_width), 'inner', axis=0, tiled=True)  35.5 us
    ppermute x7, starting transfers between devices, shards(): upper.append(lax.ppermute(upper[-1] if upper else array, 'inner', back_2))  34.9 us
    unnamed x51, local copies, waits for them, and re-layouts  29 us
    all_to_all x1, blocking collectives, shards(): lax.all_to_all(send_x, 'outer', split_axis=0, concat_axis=0, tiled=True)  19.8 us
    all_to_all x1, waiting for transfers between devices, shards(): lax.all_to_all(routed, 'outer', split_axis=0, concat_axis=0, tiled=True)  13.8 us
    dot_general x1, matrix products, shards(): lax.dot_general(up_store, up_w, (((1,), (1,)), ((), ())), preferred_eleme...  13.2 us
  transfers between devices with their start and end apart: 19, of which 11 were waited for; matrix products, arithmetic and copies ran while one was open for 18% of the time, Pallas kernels for 0%

profile of v1, /device:TPU:1, one launch (start us, length us, event | category | flops | bytes accessed | tf_op | source)
XLA Modules:
  0.0 425.3 jit_solution(10066691786194117624)
XLA Ops:
  8.3 2.3 reduce-window.6
  12.0 1.9 convolution_convert_fusion.1
  13.9 1.2 reshape.124
  15.1 19.8 %all_to_all.15 = bf16[8,6,7168]{2,1,0:T(8,128)(2,1)S(1)} all-to-all(bf16[8,6,7168]{2,1,0:T(8,128)(2,1)} %reshape.124), channel_id=1, replica_groups=mesh['outer'=8,'inner'=16] {'outer'}, dimensions={0} | all-to-all | bytes 1376256 | tf_op jit(solution)/shard_map/all_to_all | solution.py:40
  35.1 1.3 collective-permute-start
  36.4 19.7 %collective-permute-done = bf16[48,7168]{1,0:T(8,128)(2,1)S(1)} collective-permute-done((bf16[48,7168]{1,0:T(8,128)(2,1)S(1)}, bf16[48,7168]{1,0:T(8,128)(2,1)S(1)}, u32[]{:S(2)}, u32[]{:S(2)}) %collective-permute-start) | collective-permute-done | bytes 688160 | tf_op jit(solution)/shard_map/ppermute | solution.py:50
  56.9 4.8 %collective-permute-start.8 = (bf16[48,7168]{1,0:T(8,128)(2,1)S(1)}, bf16[48,7168]{1,0:T(8,128)(2,1)S(1)}, u32[]{:S(2)}, u32[]{:S(2)}) collective-permute-start(bf16[48,7168]{1,0:T(8,128)(2,1)S(1)} %reshape.125), channel_id=1, source_target_pairs={{1,0},{2,1},{3,2},{4,3},{5,4},{6,5},{7,6},{8,7},{9,8},{10,9},{11,1... | collective-permute-start | bytes 2064392 | tf_op jit(solution)/shard_map/ppermute | solution.py:52
  61.7 14.0 %collective-permute-done.1 = bf16[48,7168]{1,0:T(8,128)(2,1)S(1)} collective-permute-done((bf16[48,7168]{1,0:T(8,128)(2,1)S(1)}, bf16[48,7168]{1,0:T(8,128)(2,1)S(1)}, u32[]{:S(2)}, u32[]{:S(2)}) %collective-permute-start.1) | collective-permute-done | bytes 688160 | tf_op jit(solution)/shard_map/ppermute | solution.py:50
  76.6 4.7 %collective-permute-start.9 = (bf16[48,7168]{1,0:T(8,128)(2,1)S(1)}, bf16[48,7168]{1,0:T(8,128)(2,1)S(1)}, u32[]{:S(2)}, u32[]{:S(2)}) collective-permute-start(bf16[48,7168]{1,0:T(8,128)(2,1)S(1)} %collective-permute-done.8), channel_id=1, source_target_pairs={{1,0},{2,1},{3,2},{4,3},{5,4},{6,5},{7,6},{8,7},{9,8},{10,9},{11,1... | collective-permute-start | bytes 2064392 | tf_op jit(solution)/shard_map/ppermute | solution.py:52
  81.3 12.2 %collective-permute-done.2 = bf16[48,7168]{1,0:T(8,128)(2,1)S(1)} collective-permute-done((bf16[48,7168]{1,0:T(8,128)(2,1)S(1)}, bf16[48,7168]{1,0:T(8,128)(2,1)S(1)}, u32[]{:S(2)}, u32[]{:S(2)}) %collective-permute-start.2) | collective-permute-done | bytes 688160 | tf_op jit(solution)/shard_map/ppermute | solution.py:50
  93.6 5.3 %collective-permute-start.10 = (bf16[48,7168]{1,0:T(8,128)(2,1)S(1)}, bf16[48,7168]{1,0:T(8,128)(2,1)S(1)}, u32[]{:S(2)}, u32[]{:S(2)}) collective-permute-start(bf16[48,7168]{1,0:T(8,128)(2,1)S(1)} %collective-permute-done.9), channel_id=1, source_target_pairs={{1,0},{2,1},{3,2},{4,3},{5,4},{6,5},{7,6},{8,7},{9,8},{10,9},{11,1... | collective-permute-start | bytes 2064392 | tf_op jit(solution)/shard_map/ppermute | solution.py:52
  99.0 11.6 %collective-permute-done.3 = bf16[48,7168]{1,0:T(8,128)(2,1)S(1)} collective-permute-done((bf16[48,7168]{1,0:T(8,128)(2,1)S(1)}, bf16[48,7168]{1,0:T(8,128)(2,1)S(1)}, u32[]{:S(2)}, u32[]{:S(2)}) %collective-permute-start.3) | collective-permute-done | bytes 688160 | tf_op jit(solution)/shard_map/ppermute | solution.py:50
  110.6 5.1 %collective-permute-start.11 = (bf16[48,7168]{1,0:T(8,128)(2,1)S(1)}, bf16[48,7168]{1,0:T(8,128)(2,1)S(1)}, u32[]{:S(2)}, u32[]{:S(2)}) collective-permute-start(bf16[48,7168]{1,0:T(8,128)(2,1)S(1)} %collective-permute-done.10), channel_id=1, source_target_pairs={{1,0},{2,1},{3,2},{4,3},{5,4},{6,5},{7,6},{8,7},{9,8},{10,9},{11,1... | collective-permute-start | bytes 2064392 | tf_op jit(solution)/shard_map/ppermute | solution.py:52
  115.6 10.9 %collective-permute-done.4 = bf16[48,7168]{1,0:T(8,128)(2,1)S(1)} collective-permute-done((bf16[48,7168]{1,0:T(8,128)(2,1)S(1)}, bf16[48,7168]{1,0:T(8,128)(2,1)S(1)}, u32[]{:S(2)}, u32[]{:S(2)}) %collective-permute-start.4) | collective-permute-done | bytes 688160 | tf_op jit(solution)/shard_map/ppermute | solution.py:50
  126.6 4.8 %collective-permute-start.12 = (bf16[48,7168]{1,0:T(8,128)(2,1)S(1)}, bf16[48,7168]{1,0:T(8,128)(2,1)}, u32[]{:S(2)}, u32[]{:S(2)}) collective-permute-start(bf16[48,7168]{1,0:T(8,128)(2,1)S(1)} %collective-permute-done.11), channel_id=1, source_target_pairs={{1,0},{2,1},{3,2},{4,3},{5,4},{6,5},{7,6},{8,7},{9,8},{10,9},{11,1... | collective-permute-start | bytes 2064392 | tf_op jit(solution)/shard_map/ppermute | solution.py:52
  131.5 10.4 %collective-permute-done.5 = bf16[48,7168]{1,0:T(8,128)(2,1)} collective-permute-done((bf16[48,7168]{1,0:T(8,128)(2,1)S(1)}, bf16[48,7168]{1,0:T(8,128)(2,1)}, u32[]{:S(2)}, u32[]{:S(2)}) %collective-permute-start.5) | collective-permute-done | bytes 688160 | tf_op jit(solution)/shard_map/ppermute | solution.py:50
  142.8 4.9 %collective-permute-start.13 = (bf16[48,7168]{1,0:T(8,128)(2,1)}, bf16[48,7168]{1,0:T(8,128)(2,1)}, u32[]{:S(2)}, u32[]{:S(2)}) collective-permute-start(bf16[48,7168]{1,0:T(8,128)(2,1)} %collective-permute-done.12), channel_id=1, source_target_pairs={{1,0},{2,1},{3,2},{4,3},{5,4},{6,5},{7,6},{8,7},{9,8},{10,9},{11,1... | collective-permute-start | bytes 2064392 | tf_op jit(solution)/shard_map/ppermute | solution.py:52
  147.7 8.6 %collective-permute-done.6 = bf16[48,7168]{1,0:T(8,128)(2,1)} collective-permute-done((bf16[48,7168]{1,0:T(8,128)(2,1)}, bf16[48,7168]{1,0:T(8,128)(2,1)}, u32[]{:S(2)}, u32[]{:S(2)}) %collective-permute-start.6) | collective-permute-done | bytes 688160 | tf_op jit(solution)/shard_map/ppermute | solution.py:50
  156.3 1.9 fusion
  159.4 11.2 %all-to-all-start = ((bf16[8,6,7168]{2,1,0:T(8,128)(2,1)}), bf16[8,6,7168]{2,1,0:T(8,128)(2,1)}, u32[]{:S(2)}, u32[]{:S(2)}) async-start(bf16[8,6,7168]{2,1,0:T(8,128)(2,1)} %reshape.122), calls=%async_computation | async-start | bytes 1835008 | tf_op jit(solution)/shard_map/all_to_all | solution.py:41
  170.7 13.8 %all-to-all-done = bf16[8,6,7168]{2,1,0:T(8,128)(2,1)} async-done(((bf16[8,6,7168]{2,1,0:T(8,128)(2,1)}), bf16[8,6,7168]{2,1,0:T(8,128)(2,1)}, u32[]{:S(2)}, u32[]{:S(2)}) %all-to-all-start) | async-done | bytes 688160 | tf_op jit(solution)/shard_map/all_to_all | solution.py:41
  184.4 2.3 reshape.123
  187.1 5.3 %collective-permute-start.14 = (bf16[48,7168]{1,0:T(8,128)(2,1)}, bf16[48,7168]{1,0:T(8,128)(2,1)S(1)}, u32[]{:S(2)}, u32[]{:S(2)}) collective-permute-start(bf16[48,7168]{1,0:T(8,128)(2,1)} %collective-permute-done.13), channel_id=1, source_target_pairs={{1,0},{2,1},{3,2},{4,3},{5,4},{6,5},{7,6},{8,7},{9,8},{10,9},{11,1... | collective-permute-start | bytes 2064392 | tf_op jit(solution)/shard_map/ppermute | solution.py:52
  192.4 2.0 bitcast_dynamic-update-slice_fusion.14
  194.4 2.0 bitcast_dynamic-update-slice_fusion.13
  196.5 2.1 bitcast_dynamic-update-slice_fusion.12
  198.5 2.0 bitcast_dynamic-update-slice_fusion.11
  200.5 2.0 bitcast_dynamic-update-slice_fusion.10
  202.5 2.0 bitcast_dynamic-update-slice_fusion.9
  204.6 2.0 bitcast_dynamic-update-slice_fusion.8
  206.6 2.0 bitcast_dynamic-update-slice_fusion.7
  213.2 2.0 bitcast_dynamic-update-slice_fusion.2
  215.2 2.0 bitcast_dynamic-update-slice_fusion.1
  218.1 10.3 %gather_fusion = bf16[16,48,7168]{2,1,0:T(8,128)(2,1)} fusion(bf16[16,48,7168]{2,1,0:T(8,128)(2,1)} %bitcast_dynamic-update-slice_fusion, s32[1024]{0:T(1024)S(1)} %pad_clamp_fusion), kind=kCustom, calls=%fused_computation | custom fusion | bytes 22020160 | tf_op jit(solution)/shard_map/gather | solution.py:55
  228.4 7.2 %fusion.3 = f32[768,128]{1,0:T(8,128)S(1)} fusion(bf16[768,7168]{1,0:T(8,128)(2,1)} %bitcast.89, bf16[1,7168,128]{2,1,0:T(8,128)(2,1)S(1)} %copy-done), kind=kOutput, calls=%fused_computation.11 | convolution fusion | flops 1409286144 | bytes 13238272 | tf_op jit(solution)/shard_map/dot_general | solution.py:58
  236.4 3.0 fusion.6
  239.4 35.5 %all-gather.2.cloned.1.call-done = bf16[768,7168]{1,0:T(8,128)(2,1)} async-done(((bf16[48,7168]{1,0:T(8,128)(2,1)}), bf16[768,7168]{1,0:T(8,128)(2,1)}) %all-gather.2.cloned.1.call-update) | async-done | bytes 11010064 | tf_op jit(solution)/shard_map/all_gather | solution.py:57
  274.9 7.6 %multiply_convert_fusion.1 = (bf16[768,128]{1,0:T(8,128)(2,1)S(1)}, bf16[768,128]{1,0:T(8,128)(2,1)S(1)}) fusion(f32[768,128]{1,0:T(8,128)S(1)} %fusion.3, f32[768,128]{1,0:T(8,128)S(1)} %fusion.6, bf16[768,7168]{1,0:T(8,128)(2,1)} %all-gather.2.cloned.1.call-done, bf16[1,128,7168]{2,1,0:T(8,128)(2,1)} %param.13), kind=kOutput, calls=%fused_computation.34 | convolution fusion | flops 1410564096 | bytes 14024704 | tf_op jit(solution)/shard_map/dot_general | solution.py:63
  282.6 9.0 %fusion.1 = f32[768,7168]{1,0:T(8,128)} fusion(bf16[768,128]{1,0:T(8,128)(2,1)S(1)} %get-tuple-element.5, bf16[1,7168,128]{2,1,0:T(8,128)(2,1)S(1)} %copy-done), kind=kOutput, calls=%fused_computation.9 | convolution fusion | flops 1409286144 | bytes 24051712 | tf_op jit(solution)/shard_map/dot_general | solution.py:77
  291.6 13.2 %add_convert_fusion = bf16[768,7168]{1,0:T(8,128)(2,1)} fusion(f32[768,7168]{1,0:T(8,128)} %fusion.1, bf16[768,128]{1,0:T(8,128)(2,1)S(1)} %get-tuple-element.4, bf16[1,7168,128]{2,1,0:T(8,128)(2,1)} %param.12), kind=kOutput, calls=%fused_computation.1 | convolution fusion | flops 1420296192 | bytes 35061760 | tf_op jit(solution)/shard_map/dot_general | solution.py:83
  304.8 9.0 %convolution_bitcast_fusion.1 = f32[1,7168,128]{2,1,0:T(8,128)} fusion(bf16[768,7168]{1,0:T(8,128)(2,1)} %bitcast.90, bf16[768,128]{1,0:T(8,128)(2,1)S(1)} %get-tuple-element.4), kind=kOutput, calls=%fused_computation.3 | convolution fusion | flops 1409286144 | bytes 14876672 | tf_op jit(solution)/shard_map/dot_general | solution.py:71
  313.8 9.2 %convolution_bitcast_fusion.2 = f32[1,7168,128]{2,1,0:T(8,128)} fusion(bf16[768,7168]{1,0:T(8,128)(2,1)} %bitcast.91, bf16[768,128]{1,0:T(8,128)(2,1)S(1)} %get-tuple-element.5), kind=kOutput, calls=%fused_computation.4 | convolution fusion | flops 1409286144 | bytes 14876672 | tf_op jit(solution)/shard_map/dot_general | solution.py:70
  323.0 71.7 %reduce-scatter.2.cloned.1.call-done = bf16[48,7168]{1,0:T(8,128)(2,1)} async-done(((bf16[768,7168]{1,0:T(8,128)(2,1)}), bf16[48,7168]{1,0:T(8,128)(2,1)}) %reduce-scatter.2.cloned.1.call-update) | async-done | bytes 688144 | tf_op jit(solution)/shard_map/reduce_scatter | solution.py:80
  394.7 2.4 reshape.127
  397.1 5.5 %all-to-all-start.2 = ((bf16[8,6,7168]{2,1,0:T(8,128)(2,1)}), bf16[8,6,7168]{2,1,0:T(8,128)(2,1)S(1)}, u32[]{:S(2)}, u32[]{:S(2)}) async-start(bf16[8,6,7168]{2,1,0:T(8,128)(2,1)} %reshape.127), calls=%async_computation.3 | async-start | bytes 1835008 | tf_op jit(solution)/shard_map/all_to_all | solution.py:92
  402.6 7.7 %convolution_bitcast_fusion = f32[1,128,7168]{2,1,0:T(8,128)} fusion(bf16[768,7168]{1,0:T(8,128)(2,1)} %all-gather.2.cloned.1.call-done, f32[768,128]{1,0:T(8,128)S(1)} %fusion.6, f32[768,128]{1,0:T(8,128)S(1)} %fusion.3), kind=kOutput, calls=%fused_computation.2 | convolution fusion | flops 1409875968 | bytes 15466496 | tf_op jit(solution)/shard_map/dot_general | solution.py:72
  410.3 6.0 %all-to-all-done.2 = bf16[8,6,7168]{2,1,0:T(8,128)(2,1)S(1)} async-done(((bf16[8,6,7168]{2,1,0:T(8,128)(2,1)}), bf16[8,6,7168]{2,1,0:T(8,128)(2,1)S(1)}, u32[]{:S(2)}, u32[]{:S(2)}) %all-to-all-start.2) | async-done | bytes 688160 | tf_op jit(solution)/shard_map/all_to_all | solution.py:92
  416.6 1.9 convolution_convert_fusion
  (81 shorter events, 13.7 us)
Async XLA Ops:
  7.2 221.3 %copy-start = (bf16[1,7168,128]{2,1,0:T(8,128)(2,1)S(1)}, bf16[1,7168,128]{2,1,0:T(8,128)(2,1)}, u32[]{:S(2)}) copy-start(bf16[1,7168,128]{2,1,0:T(8,128)(2,1)} %param.11) | copy-start | bytes 5505028
  35.1 21.0 %collective-permute-start = (bf16[48,7168]{1,0:T(8,128)(2,1)S(1)}, bf16[48,7168]{1,0:T(8,128)(2,1)S(1)}, u32[]{:S(2)}, u32[]{:S(2)}) collective-permute-start(bf16[48,7168]{1,0:T(8,128)(2,1)S(1)} %reshape.125), channel_id=1, source_target_pairs={{0,1},{1,2},{2,3},{3,4},{4,5},{5,6},{6,7},{7,8},{8,9},{9,10},{10,1... | collective-permute-start | bytes 2064392 | tf_op jit(solution)/shard_map/ppermute | solution.py:50
  56.0 0.9 copy-start.4
  56.9 18.8 %collective-permute-start.1 = (bf16[48,7168]{1,0:T(8,128)(2,1)S(1)}, bf16[48,7168]{1,0:T(8,128)(2,1)S(1)}, u32[]{:S(2)}, u32[]{:S(2)}) collective-permute-start(bf16[48,7168]{1,0:T(8,128)(2,1)S(1)} %collective-permute-done), channel_id=1, source_target_pairs={{0,1},{1,2},{2,3},{3,4},{4,5},{5,6},{6,7},{7,8},{8,9},{9,10},{10,1... | collective-permute-start | bytes 2064392 | tf_op jit(solution)/shard_map/ppermute | solution.py:50
  56.9 18.8 %collective-permute-start.8 = (bf16[48,7168]{1,0:T(8,128)(2,1)S(1)}, bf16[48,7168]{1,0:T(8,128)(2,1)S(1)}, u32[]{:S(2)}, u32[]{:S(2)}) collective-permute-start(bf16[48,7168]{1,0:T(8,128)(2,1)S(1)} %reshape.125), channel_id=1, source_target_pairs={{1,0},{2,1},{3,2},{4,3},{5,4},{6,5},{7,6},{8,7},{9,8},{10,9},{11,1... | collective-permute-start | bytes 2064392 | tf_op jit(solution)/shard_map/ppermute | solution.py:52
  75.7 17.9 %copy-start.7 = (bf16[48,7168]{1,0:T(8,128)(2,1)}, bf16[48,7168]{1,0:T(8,128)(2,1)S(1)}, u32[]{:S(2)}) copy-start(bf16[48,7168]{1,0:T(8,128)(2,1)S(1)} %collective-permute-done.1) | copy-start | bytes 2064388
  75.7 17.9 %collective-permute-start.2 = (bf16[48,7168]{1,0:T(8,128)(2,1)S(1)}, bf16[48,7168]{1,0:T(8,128)(2,1)S(1)}, u32[]{:S(2)}, u32[]{:S(2)}) collective-permute-start(bf16[48,7168]{1,0:T(8,128)(2,1)S(1)} %collective-permute-done.1), channel_id=1, source_target_pairs={{0,1},{1,2},{2,3},{3,4},{4,5},{5,6},{6,7},{7,8},{8,9},{9,10},{10,1... | collective-permute-start | bytes 2064392 | tf_op jit(solution)/shard_map/ppermute | solution.py:50
  75.7 0.9 copy-start.5
  76.6 17.0 %collective-permute-start.9 = (bf16[48,7168]{1,0:T(8,128)(2,1)S(1)}, bf16[48,7168]{1,0:T(8,128)(2,1)S(1)}, u32[]{:S(2)}, u32[]{:S(2)}) collective-permute-start(bf16[48,7168]{1,0:T(8,128)(2,1)S(1)} %collective-permute-done.8), channel_id=1, source_target_pairs={{1,0},{2,1},{3,2},{4,3},{5,4},{6,5},{7,6},{8,7},{9,8},{10,9},{11,1... | collective-permute-start | bytes 2064392 | tf_op jit(solution)/shard_map/ppermute | solution.py:52
  93.6 17.0 %copy-start.10 = (bf16[48,7168]{1,0:T(8,128)(2,1)}, bf16[48,7168]{1,0:T(8,128)(2,1)S(1)}, u32[]{:S(2)}) copy-start(bf16[48,7168]{1,0:T(8,128)(2,1)S(1)} %collective-permute-done.2) | copy-start | bytes 2064388
  93.6 17.0 %collective-permute-start.3 = (bf16[48,7168]{1,0:T(8,128)(2,1)S(1)}, bf16[48,7168]{1,0:T(8,128)(2,1)S(1)}, u32[]{:S(2)}, u32[]{:S(2)}) collective-permute-start(bf16[48,7168]{1,0:T(8,128)(2,1)S(1)} %collective-permute-done.2), channel_id=1, source_target_pairs={{0,1},{1,2},{2,3},{3,4},{4,5},{5,6},{6,7},{7,8},{8,9},{9,10},{10,1... | collective-permute-start | bytes 2064392 | tf_op jit(solution)/shard_map/ppermute | solution.py:50
  93.6 5.3 %copy-start.8 = (bf16[48,7168]{1,0:T(8,128)(2,1)}, bf16[48,7168]{1,0:T(8,128)(2,1)S(1)}, u32[]{:S(2)}) copy-start(bf16[48,7168]{1,0:T(8,128)(2,1)S(1)} %collective-permute-done.9) | copy-start | bytes 2064388
  93.6 16.9 %collective-permute-start.10 = (bf16[48,7168]{1,0:T(8,128)(2,1)S(1)}, bf16[48,7168]{1,0:T(8,128)(2,1)S(1)}, u32[]{:S(2)}, u32[]{:S(2)}) collective-permute-start(bf16[48,7168]{1,0:T(8,128)(2,1)S(1)} %collective-permute-done.9), channel_id=1, source_target_pairs={{1,0},{2,1},{3,2},{4,3},{5,4},{6,5},{7,6},{8,7},{9,8},{10,9},{11,1... | collective-permute-start | bytes 2064392 | tf_op jit(solution)/shard_map/ppermute | solution.py:52
  110.5 16.1 %copy-start.15 = (bf16[48,7168]{1,0:T(8,128)(2,1)}, bf16[48,7168]{1,0:T(8,128)(2,1)S(1)}, u32[]{:S(2)}) copy-start(bf16[48,7168]{1,0:T(8,128)(2,1)S(1)} %collective-permute-done.3) | copy-start | bytes 2064388
  110.6 16.0 %collective-permute-start.4 = (bf16[48,7168]{1,0:T(8,128)(2,1)S(1)}, bf16[48,7168]{1,0:T(8,128)(2,1)S(1)}, u32[]{:S(2)}, u32[]{:S(2)}) collective-permute-start(bf16[48,7168]{1,0:T(8,128)(2,1)S(1)} %collective-permute-done.3), channel_id=1, source_target_pairs={{0,1},{1,2},{2,3},{3,4},{4,5},{5,6},{6,7},{7,8},{8,9},{9,10},{10,1... | collective-permute-start | bytes 2064392 | tf_op jit(solution)/shard_map/ppermute | solution.py:50
  110.6 5.1 %copy-start.11 = (bf16[48,7168]{1,0:T(8,128)(2,1)}, bf16[48,7168]{1,0:T(8,128)(2,1)S(1)}, u32[]{:S(2)}) copy-start(bf16[48,7168]{1,0:T(8,128)(2,1)S(1)} %collective-permute-done.10) | copy-start | bytes 2064388
  110.6 16.0 %collective-permute-start.11 = (bf16[48,7168]{1,0:T(8,128)(2,1)S(1)}, bf16[48,7168]{1,0:T(8,128)(2,1)S(1)}, u32[]{:S(2)}, u32[]{:S(2)}) collective-permute-start(bf16[48,7168]{1,0:T(8,128)(2,1)S(1)} %collective-permute-done.10), channel_id=1, source_target_pairs={{1,0},{2,1},{3,2},{4,3},{5,4},{6,5},{7,6},{8,7},{9,8},{10,9},{11,1... | collective-permute-start | bytes 2064392 | tf_op jit(solution)/shard_map/ppermute | solution.py:52
  126.6 4.9 %copy-start.16 = (bf16[48,7168]{1,0:T(8,128)(2,1)}, bf16[48,7168]{1,0:T(8,128)(2,1)S(1)}, u32[]{:S(2)}) copy-start(bf16[48,7168]{1,0:T(8,128)(2,1)S(1)} %collective-permute-done.4) | copy-start | bytes 2064388
  126.6 15.2 %collective-permute-start.5 = (bf16[48,7168]{1,0:T(8,128)(2,1)S(1)}, bf16[48,7168]{1,0:T(8,128)(2,1)}, u32[]{:S(2)}, u32[]{:S(2)}) collective-permute-start(bf16[48,7168]{1,0:T(8,128)(2,1)S(1)} %collective-permute-done.4), channel_id=1, source_target_pairs={{0,1},{1,2},{2,3},{3,4},{4,5},{5,6},{6,7},{7,8},{8,9},{9,10},{10,1... | collective-permute-start | bytes 2064392 | tf_op jit(solution)/shard_map/ppermute | solution.py:50
  126.6 29.7 %copy-start.13 = (bf16[48,7168]{1,0:T(8,128)(2,1)}, bf16[48,7168]{1,0:T(8,128)(2,1)S(1)}, u32[]{:S(2)}) copy-start(bf16[48,7168]{1,0:T(8,128)(2,1)S(1)} %collective-permute-done.11) | copy-start | bytes 2064388
  126.6 16.2 %collective-permute-start.12 = (bf16[48,7168]{1,0:T(8,128)(2,1)S(1)}, bf16[48,7168]{1,0:T(8,128)(2,1)}, u32[]{:S(2)}, u32[]{:S(2)}) collective-permute-start(bf16[48,7168]{1,0:T(8,128)(2,1)S(1)} %collective-permute-done.11), channel_id=1, source_target_pairs={{1,0},{2,1},{3,2},{4,3},{5,4},{6,5},{7,6},{8,7},{9,8},{10,9},{11,1... | collective-permute-start | bytes 2064392 | tf_op jit(solution)/shard_map/ppermute | solution.py:52
  141.8 14.5 %collective-permute-start.6 = (bf16[48,7168]{1,0:T(8,128)(2,1)}, bf16[48,7168]{1,0:T(8,128)(2,1)}, u32[]{:S(2)}, u32[]{:S(2)}) collective-permute-start(bf16[48,7168]{1,0:T(8,128)(2,1)} %collective-permute-done.5), channel_id=1, source_target_pairs={{0,1},{1,2},{2,3},{3,4},{4,5},{5,6},{6,7},{7,8},{8,9},{9,10},{10,1... | collective-permute-start | bytes 2064392 | tf_op jit(solution)/shard_map/ppermute | solution.py:50
  142.8 44.3 %collective-permute-start.13 = (bf16[48,7168]{1,0:T(8,128)(2,1)}, bf16[48,7168]{1,0:T(8,128)(2,1)}, u32[]{:S(2)}, u32[]{:S(2)}) collective-permute-start(bf16[48,7168]{1,0:T(8,128)(2,1)} %collective-permute-done.12), channel_id=1, source_target_pairs={{1,0},{2,1},{3,2},{4,3},{5,4},{6,5},{7,6},{8,7},{9,8},{10,9},{11,1... | collective-permute-start | bytes 2064392 | tf_op jit(solution)/shard_map/ppermute | solution.py:52
  156.3 36.1 %collective-permute-start.7 = (bf16[48,7168]{1,0:T(8,128)(2,1)}, bf16[48,7168]{1,0:T(8,128)(2,1)}, u32[]{:S(2)}, u32[]{:S(2)}) collective-permute-start(bf16[48,7168]{1,0:T(8,128)(2,1)} %collective-permute-done.6), channel_id=1, source_target_pairs={{0,1},{1,2},{2,3},{3,4},{4,5},{5,6},{6,7},{7,8},{8,9},{9,10},{10,1... | collective-permute-start | bytes 2064392 | tf_op jit(solution)/shard_map/ppermute | solution.py:50
  159.4 25.1 %all-to-all-start = ((bf16[8,6,7168]{2,1,0:T(8,128)(2,1)}), bf16[8,6,7168]{2,1,0:T(8,128)(2,1)}, u32[]{:S(2)}, u32[]{:S(2)}) async-start(bf16[8,6,7168]{2,1,0:T(8,128)(2,1)} %reshape.122), calls=%async_computation | async-start | bytes 1835008 | tf_op jit(solution)/shard_map/all_to_all | solution.py:41
  170.6 104.3 %all-gather.2.cloned.1.call-start = ((), (), s32[]{:S(2)}) async-start(), calls=%async_computation.4 | async-start | bytes 11698176 | tf_op jit(solution)/shard_map/all_gather | solution.py:57
  186.7 208.0 %reduce-scatter.2.cloned.1.call-start = ((), (), s32[]{:S(2)}) async-start(), calls=%async_computation.5 | async-start | bytes 11698176 | tf_op jit(solution)/shard_map/reduce_scatter | solution.py:80
  187.1 22.4 %copy-start.6 = (bf16[48,7168]{1,0:T(8,128)(2,1)S(1)}, bf16[48,7168]{1,0:T(8,128)(2,1)}, u32[]{:S(2)}) copy-start(bf16[48,7168]{1,0:T(8,128)(2,1)} %copy-done.5) | copy-start | bytes 2064388
  187.1 23.3 %copy-start.9 = (bf16[48,7168]{1,0:T(8,128)(2,1)S(1)}, bf16[48,7168]{1,0:T(8,128)(2,1)}, u32[]{:S(2)}) copy-start(bf16[48,7168]{1,0:T(8,128)(2,1)} %copy-done.8) | copy-start | bytes 2064388
  187.1 24.2 %copy-start.12 = (bf16[48,7168]{1,0:T(8,128)(2,1)S(1)}, bf16[48,7168]{1,0:T(8,128)(2,1)}, u32[]{:S(2)}) copy-start(bf16[48,7168]{1,0:T(8,128)(2,1)} %copy-done.11) | copy-start | bytes 2064388
  187.1 25.2 %copy-start.14 = (bf16[48,7168]{1,0:T(8,128)(2,1)S(1)}, bf16[48,7168]{1,0:T(8,128)(2,1)}, u32[]{:S(2)}) copy-start(bf16[48,7168]{1,0:T(8,128)(2,1)} %copy-done.13) | copy-start | bytes 2064388
  187.1 30.1 %collective-permute-start.14 = (bf16[48,7168]{1,0:T(8,128)(2,1)}, bf16[48,7168]{1,0:T(8,128)(2,1)S(1)}, u32[]{:S(2)}, u32[]{:S(2)}) collective-permute-start(bf16[48,7168]{1,0:T(8,128)(2,1)} %collective-permute-done.13), channel_id=1, source_target_pairs={{1,0},{2,1},{3,2},{4,3},{5,4},{6,5},{7,6},{8,7},{9,8},{10,9},{11,1... | collective-permute-start | bytes 2064392 | tf_op jit(solution)/shard_map/ppermute | solution.py:52
  228.4 7.4 %copy-start.2 = (bf16[16,48,7168]{2,1,0:T(8,128)(2,1)S(1)}, bf16[16,48,7168]{2,1,0:T(8,128)(2,1)}, u32[]{:S(2)}) copy-start(bf16[16,48,7168]{2,1,0:T(8,128)(2,1)} %gather_fusion) | copy-start | bytes 33030148
  228.4 8.0 %copy-start.3 = (bf16[1,7168,128]{2,1,0:T(8,128)(2,1)S(1)}, bf16[1,7168,128]{2,1,0:T(8,128)(2,1)}, u32[]{:S(2)}) copy-start(bf16[1,7168,128]{2,1,0:T(8,128)(2,1)} %param.12) | copy-start | bytes 5505028
  394.7 23.8 %copy-start.1 = (bf16[1,7168,128]{2,1,0:T(8,128)(2,1)S(1)}, bf16[1,7168,128]{2,1,0:T(8,128)(2,1)}, u32[]{:S(2)}) copy-start(bf16[1,7168,128]{2,1,0:T(8,128)(2,1)} %param.11) | copy-start | bytes 5505028
  397.1 19.2 %all-to-all-start.2 = ((bf16[8,6,7168]{2,1,0:T(8,128)(2,1)}), bf16[8,6,7168]{2,1,0:T(8,128)(2,1)S(1)}, u32[]{:S(2)}, u32[]{:S(2)}) async-start(bf16[8,6,7168]{2,1,0:T(8,128)(2,1)} %reshape.127), calls=%async_computation.3 | async-start | bytes 1835008 | tf_op jit(solution)/shard_map/all_to_all | solution.py:92
Sparse Core Ops, SparseCore 0:
  186.9 88.0 all-gather.1
  304.9 89.7 reduce-scatter.1
